TPU v7x, 32 devices: a whole 2x2x4 slice. The times are simulated.
32 devices in a mesh: fsdp: 8 (over y, x, core), dp: 4 (over z).
Axes of the slice: x: 2, y: 2, z: 4, core: 2. Of those that a mesh axis runs over, the one named last changes fastest.
Arguments:
- hidden: bfloat16 [8192, 14336], P(('fsdp', 'dp')), may hold values from -6 to 6
- cotangent: bfloat16 [8192, 4096], P(('fsdp', 'dp')), may hold values from -6 to 6
- tiles: bfloat16 [64, 128, 128], P('fsdp'), may hold values from -0.25 to 0.25
- tile_rows: int32 [64], P('fsdp'), may hold values from 0 to 111, as said below
- tile_cols: int32 [64], P('fsdp'), may hold values from 0 to 31, as said below
- counts: int32 [8], P('fsdp'), may hold values from 1 to 8, as said below
Outputs:
- layer_out: bfloat16 [8192, 4096], P(('fsdp', 'dp'))
- hidden_grad: bfloat16 [8192, 14336], P(('fsdp', 'dp'))
- weight_grad: float32 [64, 128, 128], P('fsdp')
Inputs may be any that keep to these rules, and one draw needn't show every extreme that they name: `tile_rows`: every slot (live or not) names a different block; the row block is below 112. `tile_cols`: the column block is below 32. `counts`: some owner has all 8 slots live in every draw.
All inputs are finite; a program needn't handle non-finite values.
Results may differ from a plain program's by a relative error of at most 0.0085.
Values may be sent and summed in bfloat16 or wider, within the bound.
A program may use at most 192 MiB of HBM per device.

v0:
```python
import math
import jax
import jax.numpy as jnp
from jax import lax
from jax.sharding import PartitionSpec as P


def one_hot_of(ids, width):
    return (ids[:, None] == jnp.arange(width, dtype=jnp.int32)[None, :]).astype(jnp.bfloat16)


def select_blocks(blocks, ids):
    table = one_hot_of(ids, blocks.shape[1])
    chosen = jnp.einsum("tbe,kb->tke", blocks, table, preferred_element_type=jnp.float32)
    return chosen.astype(jnp.bfloat16)


def place_blocks(partial_value, ids, width):
    table = one_hot_of(ids, width).astype(jnp.float32)
    return jnp.einsum("tke,kb->tbe", partial_value, table)


def shards(hidden, cotangent, tiles, tile_rows, tile_cols, counts):
    tokens = hidden.shape[0]
    slots_own = tiles.shape[0]
    edge_len = tiles.shape[1]
    blocks_ff = hidden.shape[1] // edge_len
    blocks_model = cotangent.shape[1] // edge_len
    live_slots = jnp.arange(slots_own) < counts[0]
    masked = jnp.where(live_slots[:, None, None], tiles, jnp.zeros_like(tiles))
    all_rows, all_cols = (
        lax.all_gather(tile_rows, "fsdp", axis=0, tiled=True),
        lax.all_gather(tile_cols, "fsdp", axis=0, tiled=True),
    )
    hidden_blocks = hidden.reshape(tokens, blocks_ff, edge_len)
    upstream_blocks = cotangent.reshape(tokens, blocks_model, edge_len)
    gathered = lax.all_gather(masked, "fsdp", axis=0, tiled=True)
    row_ids = all_rows
    col_ids = all_cols
    picked = select_blocks(hidden_blocks, row_ids)
    partial_value = jnp.einsum("tkf,kfd->tkd", picked, gathered, preferred_element_type=jnp.float32)
    layer_acc = place_blocks(partial_value, col_ids, blocks_model)
    row_ids = all_rows
    col_ids = all_cols
    upstream = select_blocks(upstream_blocks, col_ids)
    partial_value = jnp.einsum(
        "tkd,kfd->tkf", upstream, gathered, preferred_element_type=jnp.float32
    )
    grad_acc = place_blocks(partial_value, row_ids, blocks_ff)
    row_ids = all_rows
    col_ids = all_cols
    picked = select_blocks(hidden_blocks, row_ids)
    upstream = select_blocks(upstream_blocks, col_ids)
    owned = lax.psum_scatter(
        jnp.einsum("tkf,tkd->kfd", picked, upstream, preferred_element_type=jnp.float32),
        "fsdp",
        scatter_dimension=0,
        tiled=True,
    )
    summed = lax.psum(owned, "dp")
    raw_grad = jnp.where(live_slots[:, None, None], summed, jnp.zeros_like(summed))
    local_squares = jnp.sum(raw_grad * raw_grad)
    local_entries = counts[0].astype(jnp.float32) * edge_len * edge_len
    squares, entries = lax.psum((local_squares, local_entries), "fsdp")
    spread = jnp.sqrt(squares / entries)
    root_tokens = math.sqrt(tokens * lax.axis_size("fsdp") * lax.axis_size("dp"))
    factor = jnp.minimum(1.0, 0.5 * root_tokens / spread) / root_tokens
    layer_out = layer_acc.reshape(tokens, blocks_model * edge_len).astype(jnp.bfloat16)
    hidden_grad = grad_acc.reshape(tokens, blocks_ff * edge_len).astype(jnp.bfloat16)
    return (layer_out, hidden_grad, raw_grad * factor)


def solution(mesh):
    placed = (
        P(("fsdp", "dp"), None),
        P(("fsdp", "dp"), None),
        P("fsdp", None, None),
        P("fsdp"),
        P("fsdp"),
        P("fsdp"),
    )
    return jax.shard_map(
        shards,
        mesh=mesh,
        in_specs=placed,
        out_specs=(P(("fsdp", "dp"), None), P(("fsdp", "dp"), None), P("fsdp", None, None)),
        check_vma=False,
    )
```

profile of v0, /device:TPU:0, one launch (start us, length us, event | category | flops | bytes accessed | tf_op | source)
XLA Modules:
  0.0 171.5 jit_solution(11835242717945344327)
XLA Ops:
  7.9 1.7 %broadcast_select_fusion = bf16[8,128,128]{2,1,0:T(8,128)(2,1)} fusion(bf16[8,128,128]{2,1,0:T(8,128)(2,1)} %param.8, pred[8]{0:T(512)(128)(4,1)S(1)} %iota_compare_fusion.2), kind=kLoop, calls=%fused_computation.16 | loop fusion | flops 131072 | bytes 524296 | tf_op jit(solution)/shard_map/jit(_where)/select_n | solution.py:30
  9.7 7.8 %copy.16 = bf16[32,8,112,128]{3,2,1,0:T(8,128)(2,1)} copy(bf16[32,8,112,128]{3,1,2,0:T(8,128)(2,1)} %bitcast.50) | data formatting | bytes 14680064
  17.6 0.6 dynamic-slice
  18.7 0.2 dynamic-update-slice
  19.2 9.7 %all-reduce.2 = (s32[64]{0:T(128)S(1)}, s32[64]{0:T(128)S(1)}) all-reduce(s32[64]{0:T(128)S(1)} %dynamic-update-slice.1, s32[64]{0:T(128)S(1)} %dynamic-update-slice), channel_id=1, replica_groups=mesh['fsdp'=8,'dp'=4] {'fsdp'}, use_global_device_ids=true, to_apply=%add.1 | all-reduce | flops 128 | bytes 1024
  28.9 6.4 %convert_bitcast_fusion.1 = bf16[256,64,128]{2,1,0:T(8,128)(2,1)} fusion(bf16[256,112,128]{2,1,0:T(8,128)(2,1)} %bitcast.46, s32[64]{0:T(128)S(1)} %get-tuple-element.3), kind=kOutput, calls=%fused_computation.7 | convolution fusion | flops 471866368 | bytes 11534592 | tf_op jit(solution)/shard_map/tbe,kb->tke/dot_general | solution.py:14
  35.3 7.1 %copy.11 = bf16[256,64,128]{0,2,1:T(8,128)(2,1)} copy(bf16[256,64,128]{2,1,0:T(8,128)(2,1)} %convert_bitcast_fusion.1) | data formatting | bytes 8388608 | tf_op jit(solution)/shard_map/convert_element_type | solution.py:15
  42.3 0.5 copy.18
  42.8 1.3 convert_bitcast_fusion
  44.1 2.0 %copy-done.1 = bf16[256,64,128]{2,1,0:T(8,128)(2,1)} copy-done((bf16[256,64,128]{2,1,0:T(8,128)(2,1)}, bf16[256,64,128]{2,1,0:T(8,128)(2,1)S(1)}, u32[]{:S(2)}) %copy-start.1) | copy-done | bytes 4194328
  46.1 7.2 %fusion.9 = f32[64,128,128]{2,1,0:T(8,128)} fusion(bf16[256,64,128]{0,2,1:T(8,128)(2,1)S(1)} %copy-done, bf16[256,64,128]{2,1,0:T(8,128)(2,1)S(1)} %convert_bitcast_fusion), kind=kOutput, calls=%fused_computation.10 | convolution fusion | flops 536870912 | bytes 12582912 | tf_op jit(solution)/shard_map/tkf,tkd->kfd/dot_general | solution.py:55
  53.6 9.4 %fusion.7 = bf16[64,128,256]{2,1,0:T(8,128)(2,1)} fusion(bf16[64,128,128]{2,1,0:T(8,128)(2,1)} %all-gather.2.cloned.1.call-done, bf16[256,64,128]{2,1,0:T(8,128)(2,1)} %copy-done.1), kind=kOutput, calls=%fused_computation.8 | convolution fusion | flops 536870912 | bytes 10485760 | tf_op jit(solution)/shard_map/tkd,kfd->tkf/dot_general | solution.py:46
  63.0 6.6 %copy.15 = bf16[64,128,256]{1,0,2:T(8,128)(2,1)} copy(bf16[64,128,256]{2,1,0:T(8,128)(2,1)} %fusion.7) | data formatting | bytes 8388608 | tf_op jit(solution)/shard_map/tkd,kfd->tkf/dot_general | solution.py:46
  69.7 7.6 %fusion.4 = bf16[112,256,128]{2,0,1:T(8,128)(2,1)} fusion(bf16[64,128,256]{1,0,2:T(8,128)(2,1)} %copy.15, s32[64]{0:T(128)S(1)} %get-tuple-element.3), kind=kOutput, calls=%fused_computation.5 | convolution fusion | flops 469769216 | bytes 11534592 | tf_op jit(solution)/shard_map/tke,kb->tbe/dot_general | solution.py:20
  77.3 26.8 %reduce-scatter.2.cloned.1.call-done = f32[8,128,128]{2,1,0:T(8,128)} async-done(((f32[64,128,128]{2,1,0:T(8,128)}), f32[8,128,128]{2,1,0:T(8,128)}) %reduce-scatter.2.cloned.1.call-update) | async-done | bytes 524304 | tf_op jit(solution)/shard_map/reduce_scatter | solution.py:54
  104.1 5.6 %fusion.24 = bf16[64,128,256]{2,1,0:T(8,128)(2,1)} fusion(bf16[64,128,128]{2,1,0:T(8,128)(2,1)S(1)} %copy-done.3, bf16[256,64,128]{0,2,1:T(8,128)(2,1)} %copy.11), kind=kOutput, calls=%fused_computation.26 | convolution fusion | flops 536870912 | bytes 10485760 | tf_op jit(solution)/shard_map/tkf,kfd->tkd/dot_general | solution.py:41
  109.8 4.9 %copy.26 = bf16[32,8,112,128]{3,1,2,0:T(8,128)(2,1)} copy(bf16[32,8,112,128]{3,2,1,0:T(8,128)(2,1)S(1)} %bitcast.47) | data formatting | bytes 14680064
  114.7 6.5 %copy.13 = bf16[64,128,256]{1,0,2:T(8,128)(2,1)} copy(bf16[64,128,256]{2,1,0:T(8,128)(2,1)} %fusion.24) | data formatting | bytes 8388608 | tf_op jit(solution)/shard_map/tkf,kfd->tkd/dot_general | solution.py:41
  121.2 2.9 %fusion.11 = bf16[32,256,128]{2,0,1:T(8,128)(2,1)S(1)} fusion(bf16[64,128,256]{1,0,2:T(8,128)(2,1)} %copy.13, s32[64]{0:T(128)S(1)} %get-tuple-element.4), kind=kOutput, calls=%fused_computation.13 | convolution fusion | flops 134219776 | bytes 6291712 | tf_op jit(solution)/shard_map/tke,kb->tbe/dot_general | solution.py:20
  124.1 21.0 %all-reduce.6.cloned.1.call-done = f32[8,128,128]{2,1,0:T(8,128)} async-done(((f32[8,128,128]{2,1,0:T(8,128)}), f32[8,128,128]{2,1,0:T(8,128)}) %all-reduce.6.cloned.1.call-update) | async-done | bytes 524304 | tf_op jit(solution)/shard_map/psum | solution.py:60
  145.2 1.9 %multiply_reduce_fusion = f32[]{:T(128)} fusion(f32[8,128,128]{2,1,0:T(8,128)} %all-reduce.6.cloned.1.call-done, pred[8]{0:T(512)(128)(4,1)S(1)} %iota_compare_fusion.2), kind=kLoop, calls=%fused_computation.14 | loop fusion | flops 393215 | bytes 524300 | tf_op jit(solution)/shard_map/reduce_sum | solution.py:62
  147.1 2.3 %copy.27 = bf16[32,8,32,128]{3,1,2,0:T(8,128)(2,1)} copy(bf16[32,8,32,128]{3,2,1,0:T(8,128)(2,1)S(1)} %bitcast.48) | data formatting | bytes 4194304
  149.4 13.3 %all-reduce.3 = (f32[]{:T(128)}, f32[]{:T(128)}) all-reduce(f32[]{:T(128)} %multiply_reduce_fusion, f32[]{:T(128)S(6)} %mul.14), channel_id=1, replica_groups=mesh['fsdp'=8,'dp'=4] {'fsdp'}, use_global_device_ids=true, to_apply=%region_3.4 | all-reduce | flops 2 | bytes 16 | tf_op jit(solution)/shard_map/psum | solution.py:64
  164.0 0.9 select_multiply_fusion
  (28 shorter events, 0.6 us)
Async XLA Ops:
  7.2 46.5 %all-gather.2.cloned.1.call-start = ((), (), s32[]{:S(2)}) async-start(), calls=%async_computation.1 | async-start | bytes 2359296 | tf_op jit(solution)/shard_map/all_gather | solution.py:37
  9.6 94.5 %reduce-scatter.2.cloned.1.call-start = ((), (), s32[]{:S(2)}) async-start(), calls=%async_computation.2 | async-start | bytes 4718592 | tf_op jit(solution)/shard_map/reduce_scatter | solution.py:54
  9.7 7.9 %copy-start.8 = (u32[32]{0:T(128)S(1)}, u32[32]{0:T(128)}, u32[]{:S(2)}) copy-start(u32[32]{0:T(128)} %constant.18) | copy-start | bytes 388
  9.7 9.0 %copy-start.6 = (s32[8]{0:T(128)S(1)}, s32[8]{0:T(128)}, u32[]{:S(2)}) copy-start(s32[8]{0:T(128)} %param.10) | copy-start | bytes 100
  9.7 9.3 %copy-start.7 = (s32[8]{0:T(128)S(1)}, s32[8]{0:T(128)}, u32[]{:S(2)}) copy-start(s32[8]{0:T(128)} %param.9) | copy-start | bytes 100
  35.3 7.1 %copy-start.5 = (bf16[256,4096]{1,0:T(8,128)(2,1)S(1)}, bf16[256,4096]{1,0:T(8,128)(2,1)}, u32[]{:S(2)}) copy-start(bf16[256,4096]{1,0:T(8,128)(2,1)} %param.7) | copy-start | bytes 6291460
  42.8 3.3 %copy-start = (bf16[256,64,128]{0,2,1:T(8,128)(2,1)S(1)}, bf16[256,64,128]{0,2,1:T(8,128)(2,1)}, u32[]{:S(2)}) copy-start(bf16[256,64,128]{0,2,1:T(8,128)(2,1)} %copy.11) | copy-start | bytes 12582916
  44.1 2.0 %copy-start.1 = (bf16[256,64,128]{2,1,0:T(8,128)(2,1)}, bf16[256,64,128]{2,1,0:T(8,128)(2,1)S(1)}, u32[]{:S(2)}) copy-start(bf16[256,64,128]{2,1,0:T(8,128)(2,1)S(1)} %convert_bitcast_fusion) | copy-start | bytes 12582916
  53.4 91.8 %all-reduce.6.cloned.1.call-start = ((), (), s32[]{:S(2)}) async-start(), calls=%async_computation.3 | async-start | bytes 1048576 | tf_op jit(solution)/shard_map/psum | solution.py:60
  69.7 34.5 %copy-start.3 = (bf16[64,128,128]{2,1,0:T(8,128)(2,1)S(1)}, bf16[64,128,128]{2,1,0:T(8,128)(2,1)}, u32[]{:S(2)}) copy-start(bf16[64,128,128]{2,1,0:T(8,128)(2,1)} %all-gather.2.cloned.1.call-done) | copy-start | bytes 6291460
  104.1 5.6 %copy-start.2 = (bf16[112,256,128]{2,0,1:T(8,128)(2,1)S(1)}, bf16[112,256,128]{2,0,1:T(8,128)(2,1)}, u32[]{:S(2)}) copy-start(bf16[112,256,128]{2,0,1:T(8,128)(2,1)} %fusion.4) | copy-start | bytes 22020100
  145.2 18.9 %copy-start.4 = (f32[8,128,128]{2,1,0:T(8,128)S(1)}, f32[8,128,128]{2,1,0:T(8,128)}, u32[]{:S(2)}) copy-start(f32[8,128,128]{2,1,0:T(8,128)} %all-reduce.6.cloned.1.call-done) | copy-start | bytes 1572868
Sparse Core Ops, SparseCore 0:
  10.4 30.5 all-gather.1
  53.5 50.5 reduce-scatter.1
  106.4 38.6 all-reduce.5
where the time goes:
time: 172 us; the launch traced here: 171 us
  waiting for transfers between devices  47.9 us (28%)
  matrix products  40.4 us (23%)
  local copies, waits for them, and re-layouts  38.9 us (23%)
  blocking collectives  23 us (13%)
  between operations  16.4 us (10%)
  other arithmetic  4.57 us (3%)
    reduce_scatter x1, waiting for transfers between devices, shards(): lax.psum_scatter(jnp.einsum('tkf,tkd->kfd', picked, upstream, preferred_e...  26.8 us
    psum x1, waiting for transfers between devices, shards(): summed = lax.psum(owned, 'dp')  21 us
    unnamed x27, local copies, waits for them, and re-layouts  18.6 us
    psum x1, blocking collectives, shards(): squares, entries = lax.psum((local_squares, local_entries), 'fsdp')  13.3 us
    dot_general x2, matrix products, place_blocks(): return jnp.einsum('tke,kb->tbe', partial_value, table)  10.5 us
    unnamed x1, blocking collectives  9.69 us
    dot_general x1, matrix products, shards(): jnp.einsum('tkd,kfd->tkf', upstream, gathered, preferred_element_type=jnp...  9.41 us
    dot_general x2, matrix products, select_blocks(): jnp.einsum('tbe,kb->tke', blocks, table, preferred_element_type=jnp.float32)  7.66 us
  transfers between devices with their start and end apart: 3, of which 2 were waited for; matrix products, arithmetic and copies ran while one was open for 44% of the time, Pallas kernels for 0%

commit v1 on v0

--- a/solution.py
+++ b/solution.py
@@ -1,8 +1,21 @@
+import functools
 import math
 import jax
 import jax.numpy as jnp
 from jax import lax
 from jax.sharding import PartitionSpec as P
+
+
+def edit_waves(w_in, axis_tag):
+    cores_n = lax.axis_size(axis_tag)
+    tall = w_in
+    moved = lambda t1: [(dev_j, dev_j ^ t1) for dev_j in range(cores_n)]
+    for j0 in range(cores_n.bit_length() - 1):
+        tall = tall + lax.ppermute(tall, axis_tag, moved(1 << j0))
+    return tall
+
+
+answer_blocks_on = functools.partial(edit_waves, axis_tag="dp")
 
 
 def one_hot_of(ids, width):
@@ -57,7 +70,7 @@
         scatter_dimension=0,
         tiled=True,
     )
-    summed = lax.psum(owned, "dp")
+    summed = answer_blocks_on(owned)
     raw_grad = jnp.where(live_slots[:, None, None], summed, jnp.zeros_like(summed))
     local_squares = jnp.sum(raw_grad * raw_grad)
     local_entries = counts[0].astype(jnp.float32) * edge_len * edge_len

time: 172 us -> 205 us (1.19)
  waiting for transfers between devices: 47.9 us -> 84.2 us
  matrix products: 40.4 us -> 34.9 us
  starting transfers between devices: 0.3 us -> 4.22 us
    all_gather x1, waiting for transfers between devices: 0.02 us -> 28.8 us  [shards(): gathered = lax.all_gather(masked, 'fsdp', axis=0, tiled=True)]
    reduce_scatter x1, waiting for transfers between devices: 26.8 us -> 49.2 us  [shards(): lax.psum_scatter(jnp.einsum('tkf,tkd->kfd', picked, upstream, preferred_e...]
    psum x1 -> x0, waiting for transfers between devices: 21 us -> none  [shards(): summed = lax.psum(owned, 'dp')]
    ppermute x0 -> x2, waiting for transfers between devices: none -> 6.17 us  [edit_waves(): tall = tall + lax.ppermute(tall, axis_tag, moved(1 << j0))]
    ppermute x0 -> x2, starting transfers between devices: none -> 3.96 us  [edit_waves(): tall = tall + lax.ppermute(tall, axis_tag, moved(1 << j0))]
    dot_general x2, matrix products: 10.5 us -> 7.38 us  [place_blocks(): return jnp.einsum('tke,kb->tbe', partial_value, table)]
    dot_general x1, matrix products: 5.61 us -> 3.24 us  [shards(): jnp.einsum('tkf,kfd->tkd', picked, gathered, preferred_element_type=jnp.f...]
    unnamed x27 -> x29, local copies, waits for them, and re-layouts: 18.6 us -> 18.6 us
  transfers between devices with their start and end apart: 3 -> 4, of which waited for: 2 -> 3; matrix products, arithmetic and copies ran while one was open for 44% -> 19% of each run, Pallas kernels for 0% -> 0%
where the time goes in v1:
time: 205 us; the launch traced here: 204 us
  waiting for transfers between devices  84.2 us (41%)
  local copies, waits for them, and re-layouts  38.7 us (19%)
  matrix products  34.9 us (17%)
  blocking collectives  22.4 us (11%)
  between operations  16.9 us (8%)
  starting transfers between devices  4.22 us (2%)
  other arithmetic  2.57 us (1%)
    reduce_scatter x1, waiting for transfers between devices, shards(): lax.psum_scatter(jnp.einsum('tkf,tkd->kfd', picked, upstream, preferred_e...  49.2 us
    all_gather x1, waiting for transfers between devices, shards(): gathered = lax.all_gather(masked, 'fsdp', axis=0, tiled=True)  28.8 us
    unnamed x29, local copies, waits for them, and re-layouts  18.6 us
    psum x1, blocking collectives, shards(): squares, entries = lax.psum((local_squares, local_entries), 'fsdp')  12.9 us
    unnamed x1, blocking collectives  9.49 us
    dot_general x1, matrix products, shards(): jnp.einsum('tkd,kfd->tkf', upstream, gathered, preferred_element_type=jnp...  9.43 us
    dot_general x2, matrix products, select_blocks(): jnp.einsum('tbe,kb->tke', blocks, table, preferred_element_type=jnp.float32)  7.61 us
    dot_general x2, matrix products, place_blocks(): return jnp.einsum('tke,kb->tbe', partial_value, table)  7.38 us
  transfers between devices with their start and end apart: 4, of which 3 were waited for; matrix products, arithmetic and copies ran while one was open for 19% of the time, Pallas kernels for 0%

profile of v1, /device:TPU:0, one launch (start us, length us, event | category | flops | bytes accessed | tf_op | source)
XLA Modules:
  0.0 203.9 jit_solution(4988000121350219583)
XLA Ops:
  7.3 7.8 %copy.16 = bf16[32,8,112,128]{3,2,1,0:T(8,128)(2,1)} copy(bf16[32,8,112,128]{3,1,2,0:T(8,128)(2,1)} %bitcast.50) | data formatting | bytes 14680064
  16.8 9.5 %all-reduce.2 = (s32[64]{0:T(128)S(1)}, s32[64]{0:T(128)S(1)}) all-reduce(s32[64]{0:T(128)S(1)} %dynamic-update-slice.1, s32[64]{0:T(128)S(1)} %dynamic-update-slice), channel_id=1, replica_groups=mesh['fsdp'=8,'dp'=4] {'fsdp'}, use_global_device_ids=true, to_apply=%add.1 | all-reduce | flops 128 | bytes 1024
  26.3 6.3 %convert_bitcast_fusion.1 = bf16[256,64,128]{2,1,0:T(8,128)(2,1)} fusion(bf16[256,112,128]{2,1,0:T(8,128)(2,1)} %bitcast.46, s32[64]{0:T(128)S(1)} %get-tuple-element.3), kind=kOutput, calls=%fused_computation.7 | convolution fusion | flops 471866368 | bytes 11534592 | tf_op jit(solution)/shard_map/tbe,kb->tke/dot_general | solution.py:27
  32.6 7.0 %copy.11 = bf16[256,64,128]{0,2,1:T(8,128)(2,1)} copy(bf16[256,64,128]{2,1,0:T(8,128)(2,1)} %convert_bitcast_fusion.1) | data formatting | bytes 8388608 | tf_op jit(solution)/shard_map/convert_element_type | solution.py:28
  40.1 1.3 convert_bitcast_fusion
  41.4 1.9 copy-done.2
  43.3 7.2 %fusion.9 = f32[64,128,128]{2,1,0:T(8,128)} fusion(bf16[256,64,128]{0,2,1:T(8,128)(2,1)S(1)} %copy-done, bf16[256,64,128]{2,1,0:T(8,128)(2,1)S(1)} %convert_bitcast_fusion), kind=kOutput, calls=%fused_computation.10 | convolution fusion | flops 536870912 | bytes 12582912 | tf_op jit(solution)/shard_map/tkf,tkd->kfd/dot_general | solution.py:68
  51.5 0.8 broadcast_select_fusion
  52.3 49.2 %reduce-scatter.2.cloned.1.call-done = f32[8,128,128]{2,1,0:T(8,128)} async-done(((f32[64,128,128]{2,1,0:T(8,128)}), f32[8,128,128]{2,1,0:T(8,128)}) %reduce-scatter.2.cloned.1.call-update) | async-done | bytes 524304 | tf_op jit(solution)/shard_map/reduce_scatter | solution.py:67
  101.6 1.5 collective-permute-start
  103.1 28.8 %all-gather.2.cloned.1.call-done = bf16[64,128,128]{2,1,0:T(8,128)(2,1)} async-done(((bf16[8,128,128]{2,1,0:T(8,128)(2,1)}), bf16[64,128,128]{2,1,0:T(8,128)(2,1)}) %all-gather.2.cloned.1.call-update) | async-done | bytes 2097168 | tf_op jit(solution)/shard_map/all_gather | solution.py:50
  131.8 9.4 %fusion.7 = bf16[64,128,256]{2,1,0:T(8,128)(2,1)} fusion(bf16[64,128,128]{2,1,0:T(8,128)(2,1)} %all-gather.2.cloned.1.call-done, bf16[256,64,128]{2,1,0:T(8,128)(2,1)} %copy-done.2), kind=kOutput, calls=%fused_computation.8 | convolution fusion | flops 536870912 | bytes 10485760 | tf_op jit(solution)/shard_map/tkd,kfd->tkf/dot_general | solution.py:59
  141.3 6.6 %copy.15 = bf16[64,128,256]{1,0,2:T(8,128)(2,1)} copy(bf16[64,128,256]{2,1,0:T(8,128)(2,1)} %fusion.7) | data formatting | bytes 8388608 | tf_op jit(solution)/shard_map/tkd,kfd->tkf/dot_general | solution.py:59
  147.8 4.5 %fusion.4 = bf16[112,256,128]{2,0,1:T(8,128)(2,1)S(1)} fusion(bf16[64,128,256]{1,0,2:T(8,128)(2,1)} %copy.15, s32[64]{0:T(128)S(1)} %get-tuple-element.3), kind=kOutput, calls=%fused_computation.5 | convolution fusion | flops 469769216 | bytes 11534592 | tf_op jit(solution)/shard_map/tke,kb->tbe/dot_general | solution.py:33
  152.4 2.5 %collective-permute-start.1 = (f32[8,128,128]{2,1,0:T(8,128)S(1)}, f32[8,128,128]{2,1,0:T(8,128)S(1)}, u32[]{:S(2)}, u32[]{:S(2)}) collective-permute-start(f32[8,128,128]{2,1,0:T(8,128)S(1)} %add.12), channel_id=1, source_target_pairs={{0,2},{1,3},{2,0},{3,1},{4,6},{5,7},{6,4},{7,5},{8,10},{9,11},{10,... | collective-permute-start | bytes 1572872 | tf_op jit(solution)/shard_map/ppermute | solution.py:14
  154.9 3.2 %fusion.24 = bf16[64,128,256]{2,1,0:T(8,128)(2,1)} fusion(bf16[64,128,128]{2,1,0:T(8,128)(2,1)S(1)} %copy-done.3, bf16[256,64,128]{0,2,1:T(8,128)(2,1)S(1)} %copy-done.1), kind=kOutput, calls=%fused_computation.27 | convolution fusion | flops 536870912 | bytes 10485760 | tf_op jit(solution)/shard_map/tkf,kfd->tkd/dot_general | solution.py:54
  158.1 4.9 %copy.26 = bf16[32,8,112,128]{3,1,2,0:T(8,128)(2,1)} copy(bf16[32,8,112,128]{3,2,1,0:T(8,128)(2,1)S(1)} %bitcast.47) | data formatting | bytes 14680064
  163.1 6.6 %copy.13 = bf16[64,128,256]{1,0,2:T(8,128)(2,1)} copy(bf16[64,128,256]{2,1,0:T(8,128)(2,1)} %fusion.24) | data formatting | bytes 8388608 | tf_op jit(solution)/shard_map/tkf,kfd->tkd/dot_general | solution.py:54
  169.6 2.9 %fusion.11 = bf16[32,256,128]{2,0,1:T(8,128)(2,1)S(1)} fusion(bf16[64,128,256]{1,0,2:T(8,128)(2,1)} %copy.13, s32[64]{0:T(128)S(1)} %get-tuple-element.4), kind=kOutput, calls=%fused_computation.13 | convolution fusion | flops 134219776 | bytes 6291712 | tf_op jit(solution)/shard_map/tke,kb->tbe/dot_general | solution.py:33
  172.5 6.2 %collective-permute-done.1 = f32[8,128,128]{2,1,0:T(8,128)S(1)} collective-permute-done((f32[8,128,128]{2,1,0:T(8,128)S(1)}, f32[8,128,128]{2,1,0:T(8,128)S(1)}, u32[]{:S(2)}, u32[]{:S(2)}) %collective-permute-start.1) | collective-permute-done | bytes 524320 | tf_op jit(solution)/shard_map/ppermute | solution.py:14
  178.7 0.8 multiply_reduce_fusion
  179.5 2.3 %copy.27 = bf16[32,8,32,128]{3,1,2,0:T(8,128)(2,1)} copy(bf16[32,8,32,128]{3,2,1,0:T(8,128)(2,1)S(1)} %bitcast.48) | data formatting | bytes 4194304
  181.8 12.9 %all-reduce.3 = (f32[]{:T(128)}, f32[]{:T(128)}) all-reduce(f32[]{:T(128)} %multiply_reduce_fusion, f32[]{:T(128)S(6)} %mul.14), channel_id=1, replica_groups=mesh['fsdp'=8,'dp'=4] {'fsdp'}, use_global_device_ids=true, to_apply=%region_2.3 | all-reduce | flops 2 | bytes 16 | tf_op jit(solution)/shard_map/psum | solution.py:77
  196.1 0.9 broadcast_multiply_fusion
  (32 shorter events, 2.0 us)
Async XLA Ops:
  7.2 94.4 %reduce-scatter.2.cloned.1.call-start = ((), (), s32[]{:S(2)}) async-start(), calls=%async_computation.2 | async-start | bytes 4718592 | tf_op jit(solution)/shard_map/reduce_scatter | solution.py:67
  7.2 7.9 %copy-start.9 = (u32[32]{0:T(128)S(1)}, u32[32]{0:T(128)}, u32[]{:S(2)}) copy-start(u32[32]{0:T(128)} %constant.18) | copy-start | bytes 388
  7.2 9.1 %copy-start.7 = (s32[8]{0:T(128)S(1)}, s32[8]{0:T(128)}, u32[]{:S(2)}) copy-start(s32[8]{0:T(128)} %param.10) | copy-start | bytes 100
  7.2 9.4 %copy-start.8 = (s32[8]{0:T(128)S(1)}, s32[8]{0:T(128)}, u32[]{:S(2)}) copy-start(s32[8]{0:T(128)} %param.9) | copy-start | bytes 100
  32.6 7.0 %copy-start.4 = (bf16[256,4096]{1,0:T(8,128)(2,1)S(1)}, bf16[256,4096]{1,0:T(8,128)(2,1)}, u32[]{:S(2)}) copy-start(bf16[256,4096]{1,0:T(8,128)(2,1)} %param.7) | copy-start | bytes 6291460
  40.1 3.3 %copy-start = (bf16[256,64,128]{0,2,1:T(8,128)(2,1)S(1)}, bf16[256,64,128]{0,2,1:T(8,128)(2,1)}, u32[]{:S(2)}) copy-start(bf16[256,64,128]{0,2,1:T(8,128)(2,1)} %copy.11) | copy-start | bytes 12582916
  41.4 1.9 copy-start.2
  50.5 0.9 copy-start.6
  50.6 81.3 %all-gather.2.cloned.1.call-start = ((), (), s32[]{:S(2)}) async-start(), calls=%async_computation.1 | async-start | bytes 2359296 | tf_op jit(solution)/shard_map/all_gather | solution.py:50
  101.6 50.8 %collective-permute-start = (f32[8,128,128]{2,1,0:T(8,128)}, f32[8,128,128]{2,1,0:T(8,128)S(1)}, u32[]{:S(2)}, u32[]{:S(2)}) collective-permute-start(f32[8,128,128]{2,1,0:T(8,128)} %reduce-scatter.2.cloned.1.call-done), channel_id=1, source_target_pairs={{0,1},{1,0},{2,3},{3,2},{4,5},{5,4},{6,7},{7,6},{8,9},{9,8},{10,11... | collective-permute-start | bytes 1572872 | tf_op jit(solution)/shard_map/ppermute | solution.py:14
  147.8 4.5 %copy-start.5 = (f32[8,128,128]{2,1,0:T(8,128)S(1)}, f32[8,128,128]{2,1,0:T(8,128)}, u32[]{:S(2)}) copy-start(f32[8,128,128]{2,1,0:T(8,128)} %reduce-scatter.2.cloned.1.call-done) | copy-start | bytes 1572868
  147.8 7.1 %copy-start.1 = (bf16[256,64,128]{0,2,1:T(8,128)(2,1)S(1)}, bf16[256,64,128]{0,2,1:T(8,128)(2,1)}, u32[]{:S(2)}) copy-start(bf16[256,64,128]{0,2,1:T(8,128)(2,1)} %copy.11) | copy-start | bytes 12582916
  147.8 7.1 %copy-start.3 = (bf16[64,128,128]{2,1,0:T(8,128)(2,1)S(1)}, bf16[64,128,128]{2,1,0:T(8,128)(2,1)}, u32[]{:S(2)}) copy-start(bf16[64,128,128]{2,1,0:T(8,128)(2,1)} %all-gather.2.cloned.1.call-done) | copy-start | bytes 6291460
  152.4 26.3 %collective-permute-start.1 = (f32[8,128,128]{2,1,0:T(8,128)S(1)}, f32[8,128,128]{2,1,0:T(8,128)S(1)}, u32[]{:S(2)}, u32[]{:S(2)}) collective-permute-start(f32[8,128,128]{2,1,0:T(8,128)S(1)} %add.12), channel_id=1, source_target_pairs={{0,2},{1,3},{2,0},{3,1},{4,6},{5,7},{6,4},{7,5},{8,10},{9,11},{10,... | collective-permute-start | bytes 1572872 | tf_op jit(solution)/shard_map/ppermute | solution.py:14
Sparse Core Ops, SparseCore 0:
  50.7 50.8 reduce-scatter.1
  104.0 27.7 all-gather.1
